TPU v7x, 256 devices: a whole 4x4x8 slice. The times are simulated.
256 devices in a mesh: lat: 8 (over z), lon: 32 (over x, y, core).
Axes of the slice: x: 4, y: 4, z: 8, core: 2. Of those that a mesh axis runs over, the one named last changes fastest.
Arguments:
- inputs: bfloat16 [4, 128, 256, 1024], P(None, 'lat', 'lon'), may hold values from -6 to 6
- w_reduce: bfloat16 [1024, 256], replicated, may hold values from -0.1875 to 0.1875
- gain_reduce: float32 [256], replicated, may hold values from 0.1 to 1.9
- bias_reduce: float32 [256], replicated, may hold values from -3 to 3
- w_dilated: bfloat16 [3, 3, 256, 256], replicated, may hold values from -0.125 to 0.125
- gain_dilated: float32 [256], replicated, may hold values from 0.1 to 1.9
- bias_dilated: float32 [256], replicated, may hold values from -3 to 3
- w_expand: bfloat16 [256, 1024], replicated, may hold values from -0.375 to 0.375
- gain_expand: float32 [1024], replicated, may hold values from 0.1 to 1.9
- bias_expand: float32 [1024], replicated, may hold values from -3 to 3
- grad_out: bfloat16 [4, 128, 256, 1024], P(None, 'lat', 'lon'), may hold values from -6 to 6
- labels: int32 [4, 128, 256], P(None, 'lat', 'lon'), may hold values from 0 to 2
- class_weight: float32 [3], replicated, may hold values from 0.5 to 8
Outputs:
- grad_inputs: bfloat16 [4, 128, 256, 1024], P(None, 'lat', 'lon')
- grad_reduce: bfloat16 [1024, 256], replicated
- grad_dilated: bfloat16 [3, 3, 256, 256], replicated
- grad_expand: bfloat16 [256, 1024], replicated
All inputs are finite; a program needn't handle non-finite values.
Results may differ from a plain program's by a relative error of at most 0.0079.
Values may be sent and summed in bfloat16 or wider, within the bound.
A program may use at most 64 MiB of HBM per device.

v0:
```python
import jax
import jax.numpy as jnp
from jax import lax
from jax.sharding import PartitionSpec as P


def with_halo(cells, sides, width, closed):
    for axis, dim in sides:
        count = lax.axis_size(axis)
        ends = count if closed else count - 1
        head = lax.slice_in_dim(cells, 0, width, axis=dim)
        tail = lax.slice_in_dim(cells, cells.shape[dim] - width, cells.shape[dim], axis=dim)
        cells = jnp.concatenate(
            [
                lax.ppermute(tail, axis, [(i, (i + 1) % count) for i in range(ends)]),
                cells,
                lax.ppermute(head, axis, [((i + 1) % count, i) for i in range(ends)]),
            ],
            axis=dim,
        )
    return cells


def smooth(pre):
    return pre * jax.nn.sigmoid(pre)


def slope(pre):
    sig = jax.nn.sigmoid(pre)
    return sig * (1.0 + pre * (1.0 - sig))


def gather_taps(padded, height, width, flipped):
    pieces = []
    for row_tap in range(3):
        for col_tap in range(3):
            off_row = 4 - 2 * row_tap if flipped else 2 * row_tap
            off_col = 4 - 2 * col_tap if flipped else 2 * col_tap
            pieces.append(padded[:, off_row : off_row + height, off_col : off_col + width, :])
    stacked = jnp.concatenate(pieces, axis=-1)
    return stacked.reshape(-1, stacked.shape[-1])


def pixel_sum(left, right):
    return lax.dot_general(
        left, right, (((0,), (0,)), ((), ())), preferred_element_type=jnp.float32
    )


def per_device(
    inputs,
    w_reduce,
    gain_reduce,
    bias_reduce,
    w_dilated,
    gain_dilated,
    bias_dilated,
    w_expand,
    gain_expand,
    bias_expand,
    grad_out,
    labels,
    class_weight,
):
    batch, height, width, chan_in = inputs.shape
    chan_mid = w_reduce.shape[1]
    pixels = batch * height * width
    kernel = w_dilated.reshape(9 * chan_mid, chan_mid)
    kernel_back = jnp.transpose(w_dilated, (0, 1, 3, 2)).reshape(9 * chan_mid, chan_mid)
    classes = jnp.arange(class_weight.shape[0], dtype=jnp.int32)
    flat_in = inputs.reshape(pixels, chan_in)
    pre_one = (
        jnp.dot(flat_in, w_reduce, preferred_element_type=jnp.float32) * gain_reduce + bias_reduce
    )
    mid_one = smooth(pre_one).astype(jnp.bfloat16).reshape(batch, height, width, chan_mid)
    rows_one = with_halo(mid_one, (("lat", 1),), 2, False)
    padded_one = with_halo(rows_one, (("lon", 2),), 2, True)
    taps_one = gather_taps(padded_one, height, width, False)
    pre_two = (
        jnp.dot(taps_one, kernel, preferred_element_type=jnp.float32) * gain_dilated + bias_dilated
    )
    mid_two = smooth(pre_two).astype(jnp.bfloat16)
    pre_three = (
        jnp.dot(mid_two, w_expand, preferred_element_type=jnp.float32) * gain_expand
        + bias_expand
        + flat_in.astype(jnp.float32)
    )
    pixel_weight = jnp.sum(
        jnp.where(labels.reshape(pixels, 1) == classes, class_weight, 0.0), axis=-1
    )
    grad_full = (
        grad_out.reshape(pixels, chan_in).astype(jnp.float32)
        * pixel_weight[:, None]
        * slope(pre_three)
    )
    grad_three = (grad_full * gain_expand).astype(jnp.bfloat16)
    term_expand = pixel_sum(mid_two, grad_three)
    grad_two = (
        jnp.dot(grad_three, w_expand.T, preferred_element_type=jnp.float32)
        * slope(pre_two)
        * gain_dilated
    ).astype(jnp.bfloat16)
    term_dilated = pixel_sum(taps_one, grad_two)
    rows_two = with_halo(grad_two.reshape(batch, height, width, chan_mid), (("lat", 1),), 2, False)
    padded_two = with_halo(rows_two, (("lon", 2),), 2, True)
    taps_two = gather_taps(padded_two, height, width, True)
    grad_one = (
        jnp.dot(taps_two, kernel_back, preferred_element_type=jnp.float32)
        * slope(pre_one)
        * gain_reduce
    ).astype(jnp.bfloat16)
    term_reduce = pixel_sum(flat_in, grad_one)
    grad_inputs = (
        jnp.dot(grad_one, w_reduce.T, preferred_element_type=jnp.float32) + grad_full
    ).astype(jnp.bfloat16)
    total_reduce, total_dilated, total_expand = lax.psum(
        (term_reduce, term_dilated, term_expand), ("lat", "lon")
    )
    grad_reduce = total_reduce.astype(jnp.bfloat16)
    grad_dilated = total_dilated.astype(jnp.bfloat16)
    grad_expand = total_expand.astype(jnp.bfloat16)
    grad_dilated = grad_dilated.reshape(3, 3, chan_mid, chan_mid)
    return (
        grad_inputs.reshape(batch, height, width, chan_in),
        grad_reduce,
        grad_dilated,
        grad_expand,
    )


def solution(mesh):
    return jax.shard_map(
        per_device,
        mesh=mesh,
        in_specs=(
            P(None, "lat", "lon", None),
            P(),
            P(),
            P(),
            P(),
            P(),
            P(),
            P(),
            P(),
            P(),
            P(None, "lat", "lon", None),
            P(None, "lat", "lon"),
            P(),
        ),
        out_specs=(P(None, "lat", "lon", None), P(), P(), P()),
        check_vma=False,
    )
```

profile of v0, /device:TPU:1, one launch (start us, length us, event | category | flops | bytes accessed | tf_op | source)
XLA Modules:
  0.0 187.2 jit_solution(14700682848667514248)
XLA Ops:
  0.6 1.0 copy-done
  1.7 1.8 multiply_convert_fusion.2
  3.5 4.4 %collective-permute-start = (bf16[4,2,8,256]{3,2,1,0:T(8,128)(2,1)S(1)}, bf16[4,2,8,256]{3,2,1,0:T(8,128)(2,1)S(1)}, u32[]{:S(2)}, u32[]{:S(2)}) collective-permute-start(bf16[4,2,8,256]{3,2,1,0:T(8,128)(2,1)S(1)} %get-tuple-element.45), channel_id=1, source_target_pairs={{0,32},{32,64},{64,96},{96,128},{128,160},{160,192},{192,224},{1,3... | collective-permute-start | bytes 98312 | tf_op jit(solution)/shard_map/ppermute | solution.py:15
  7.9 1.3 collective-permute-start.1
  9.5 1.5 copy.22
  11.0 1.7 collective-permute-done.1
  12.8 3.2 %collective-permute-start.2 = (bf16[4,20,2,256]{3,2,1,0:T(2,128)(2,1)S(1)}, bf16[4,20,2,256]{3,2,1,0:T(2,128)(2,1)S(1)}, u32[]{:S(2)}, u32[]{:S(2)}) collective-permute-start(bf16[4,20,2,256]{3,2,1,0:T(2,128)(2,1)S(1)} %get-tuple-element.38), channel_id=1, source_target_pairs={{0,1},{1,2},{2,3},{3,4},{4,5},{5,6},{6,7},{7,8},{8,9},{9,10},{10,1... | collective-permute-start | bytes 245768 | tf_op jit(solution)/shard_map/ppermute | solution.py:15
  16.1 1.4 collective-permute-done.2
  17.5 2.7 %collective-permute-done.3 = bf16[4,20,2,256]{3,2,1,0:T(2,128)(2,1)S(1)} collective-permute-done((bf16[4,20,2,256]{3,2,1,0:T(2,128)(2,1)S(1)}, bf16[4,20,2,256]{3,2,1,0:T(2,128)(2,1)S(1)}, u32[]{:S(2)}, u32[]{:S(2)}) %collective-permute-start.3) | collective-permute-done | bytes 81952 | tf_op jit(solution)/shard_map/ppermute | solution.py:17
  20.2 0.4 pad_maximum_fusion
  20.6 0.2 fusion.10
  21.0 0.4 copy-done.10
  21.5 0.8 fusion.2
  22.3 0.4 copy-done.3
  22.7 0.3 copy-done.7
  23.1 1.3 fusion
  24.4 0.5 fusion.6
  25.0 0.8 fusion.14
  25.8 3.5 %collective-permute-start.4 = (bf16[4,2,8,256]{3,2,1,0:T(8,128)(2,1)S(1)}, bf16[4,2,8,256]{3,2,1,0:T(8,128)(2,1)S(1)}, u32[]{:S(2)}, u32[]{:S(2)}) collective-permute-start(bf16[4,2,8,256]{3,2,1,0:T(8,128)(2,1)S(1)} %get-tuple-element.41), channel_id=1, source_target_pairs={{0,32},{32,64},{64,96},{96,128},{128,160},{160,192},{192,224},{1,3... | collective-permute-start | bytes 98312 | tf_op jit(solution)/shard_map/ppermute | solution.py:15
  29.4 1.3 collective-permute-start.5
  30.7 1.5 fusion.7
  32.2 3.1 %collective-permute-done.5 = bf16[4,2,8,256]{3,2,1,0:T(8,128)(2,1)S(1)} collective-permute-done((bf16[4,2,8,256]{3,2,1,0:T(8,128)(2,1)S(1)}, bf16[4,2,8,256]{3,2,1,0:T(8,128)(2,1)S(1)}, u32[]{:S(2)}, u32[]{:S(2)}) %collective-permute-start.5) | collective-permute-done | bytes 32800 | tf_op jit(solution)/shard_map/ppermute | solution.py:17
  35.4 3.1 %collective-permute-start.6 = (bf16[4,20,2,256]{3,2,1,0:T(2,128)(2,1)S(1)}, bf16[4,20,2,256]{3,2,1,0:T(2,128)(2,1)S(1)}, u32[]{:S(2)}, u32[]{:S(2)}) collective-permute-start(bf16[4,20,2,256]{3,2,1,0:T(2,128)(2,1)S(1)} %get-tuple-element.34), channel_id=1, source_target_pairs={{1,0},{2,1},{3,2},{4,3},{5,4},{6,5},{7,6},{8,7},{9,8},{10,9},{11,1... | collective-permute-start | bytes 245768 | tf_op jit(solution)/shard_map/ppermute | solution.py:17
  38.5 0.9 collective-permute-done.6
  39.4 3.8 %collective-permute-done.7 = bf16[4,20,2,256]{3,2,1,0:T(2,128)(2,1)S(1)} collective-permute-done((bf16[4,20,2,256]{3,2,1,0:T(2,128)(2,1)S(1)}, bf16[4,20,2,256]{3,2,1,0:T(2,128)(2,1)S(1)}, u32[]{:S(2)}, u32[]{:S(2)}) %collective-permute-start.7) | collective-permute-done | bytes 81952 | tf_op jit(solution)/shard_map/ppermute | solution.py:15
  43.2 0.4 maximum_maximum_fusion.1
  44.0 1.0 copy-done.2
  45.1 0.8 fusion.5
  45.9 1.5 convolution_bitcast_fusion
  47.4 1.5 add_convert_fusion
  48.8 137.4 %all-reduce.2 = (bf16[1024,256]{0,1:T(8,128)(2,1)S(1)}, bf16[2304,256]{1,0:T(8,128)(2,1)}, bf16[256,1024]{1,0:T(8,128)(2,1)}) all-reduce(f32[1024,256]{0,1:T(8,128)} %convolution_bitcast_fusion, f32[2304,256]{1,0:T(8,128)S(1)} %fusion.14, f32[256,1024]{1,0:T(8,128)} %fusion.7), channel_id=1, replica_groups=mesh['lat'=8,'lon'=32] {'lat','lon'}, use_global_device_ids=true, to_apply=%region_1.2 | all-reduce | flops 1114112 | bytes 6684672 | tf_op jit(solution)/shard_map/psum | solution.py:116
  186.2 1.0 copy.23
  (54 shorter events, 1.3 us)
Async XLA Ops:
  0.6 1.0 copy-start
  1.7 7.5 %copy-start.4 = (s32[4,16,8]{1,2,0:T(8,128)S(1)}, s32[4,16,8]{1,2,0:T(8,128)}, u32[]{:S(2)}) copy-start(s32[4,16,8]{1,2,0:T(8,128)} %param.24) | copy-start | bytes 6148
  1.7 7.7 %copy-start.6 = (f32[3]{0:T(128)S(1)}, f32[3]{0:T(128)}, u32[]{:S(2)}) copy-start(f32[3]{0:T(128)} %param.25) | copy-start | bytes 40
  1.7 7.8 %copy-start.1 = (bf16[3,3,256,256]{3,2,1,0:T(8,128)(2,1)S(1)}, bf16[3,3,256,256]{3,2,1,0:T(8,128)(2,1)}, u32[]{:S(2)}) copy-start(bf16[3,3,256,256]{3,2,1,0:T(8,128)(2,1)} %param.17) | copy-start | bytes 3538948
  3.5 7.5 %collective-permute-start = (bf16[4,2,8,256]{3,2,1,0:T(8,128)(2,1)S(1)}, bf16[4,2,8,256]{3,2,1,0:T(8,128)(2,1)S(1)}, u32[]{:S(2)}, u32[]{:S(2)}) collective-permute-start(bf16[4,2,8,256]{3,2,1,0:T(8,128)(2,1)S(1)} %get-tuple-element.45), channel_id=1, source_target_pairs={{0,32},{32,64},{64,96},{96,128},{128,160},{160,192},{192,224},{1,3... | collective-permute-start | bytes 98312 | tf_op jit(solution)/shard_map/ppermute | solution.py:15
  7.9 4.8 %collective-permute-start.1 = (bf16[4,2,8,256]{3,2,1,0:T(8,128)(2,1)S(1)}, bf16[4,2,8,256]{3,2,1,0:T(8,128)(2,1)S(1)}, u32[]{:S(2)}, u32[]{:S(2)}) collective-permute-start(bf16[4,2,8,256]{3,2,1,0:T(8,128)(2,1)S(1)} %get-tuple-element.46), channel_id=1, source_target_pairs={{32,0},{64,32},{96,64},{128,96},{160,128},{192,160},{224,192},{33,... | collective-permute-start | bytes 98312 | tf_op jit(solution)/shard_map/ppermute | solution.py:17
  12.8 4.7 %collective-permute-start.2 = (bf16[4,20,2,256]{3,2,1,0:T(2,128)(2,1)S(1)}, bf16[4,20,2,256]{3,2,1,0:T(2,128)(2,1)S(1)}, u32[]{:S(2)}, u32[]{:S(2)}) collective-permute-start(bf16[4,20,2,256]{3,2,1,0:T(2,128)(2,1)S(1)} %get-tuple-element.38), channel_id=1, source_target_pairs={{0,1},{1,2},{2,3},{3,4},{4,5},{5,6},{6,7},{7,8},{8,9},{9,10},{10,1... | collective-permute-start | bytes 245768 | tf_op jit(solution)/shard_map/ppermute | solution.py:15
  16.0 4.2 %collective-permute-start.3 = (bf16[4,20,2,256]{3,2,1,0:T(2,128)(2,1)S(1)}, bf16[4,20,2,256]{3,2,1,0:T(2,128)(2,1)S(1)}, u32[]{:S(2)}, u32[]{:S(2)}) collective-permute-start(bf16[4,20,2,256]{3,2,1,0:T(2,128)(2,1)S(1)} %get-tuple-element.37), channel_id=1, source_target_pairs={{1,0},{2,1},{3,2},{4,3},{5,4},{6,5},{7,6},{8,7},{9,8},{10,9},{11,1... | collective-permute-start | bytes 245768 | tf_op jit(solution)/shard_map/ppermute | solution.py:17
  20.8 0.7 copy-start.10
  20.8 0.7 copy-start.11
  21.5 1.2 copy-start.3
  21.5 1.2 copy-start.5
  21.5 1.6 copy-start.7
  21.5 1.7 copy-start.8
  21.5 1.7 copy-start.9
  25.8 6.4 %collective-permute-start.4 = (bf16[4,2,8,256]{3,2,1,0:T(8,128)(2,1)S(1)}, bf16[4,2,8,256]{3,2,1,0:T(8,128)(2,1)S(1)}, u32[]{:S(2)}, u32[]{:S(2)}) collective-permute-start(bf16[4,2,8,256]{3,2,1,0:T(8,128)(2,1)S(1)} %get-tuple-element.41), channel_id=1, source_target_pairs={{0,32},{32,64},{64,96},{96,128},{128,160},{160,192},{192,224},{1,3... | collective-permute-start | bytes 98312 | tf_op jit(solution)/shard_map/ppermute | solution.py:15
  29.4 5.9 %collective-permute-start.5 = (bf16[4,2,8,256]{3,2,1,0:T(8,128)(2,1)S(1)}, bf16[4,2,8,256]{3,2,1,0:T(8,128)(2,1)S(1)}, u32[]{:S(2)}, u32[]{:S(2)}) collective-permute-start(bf16[4,2,8,256]{3,2,1,0:T(8,128)(2,1)S(1)} %get-tuple-element.42), channel_id=1, source_target_pairs={{32,0},{64,32},{96,64},{128,96},{160,128},{192,160},{224,192},{33,... | collective-permute-start | bytes 98312 | tf_op jit(solution)/shard_map/ppermute | solution.py:17
  35.4 4.0 %collective-permute-start.6 = (bf16[4,20,2,256]{3,2,1,0:T(2,128)(2,1)S(1)}, bf16[4,20,2,256]{3,2,1,0:T(2,128)(2,1)S(1)}, u32[]{:S(2)}, u32[]{:S(2)}) collective-permute-start(bf16[4,20,2,256]{3,2,1,0:T(2,128)(2,1)S(1)} %get-tuple-element.34), channel_id=1, source_target_pairs={{1,0},{2,1},{3,2},{4,3},{5,4},{6,5},{7,6},{8,7},{9,8},{10,9},{11,1... | collective-permute-start | bytes 245768 | tf_op jit(solution)/shard_map/ppermute | solution.py:17
  38.5 4.7 %collective-permute-start.7 = (bf16[4,20,2,256]{3,2,1,0:T(2,128)(2,1)S(1)}, bf16[4,20,2,256]{3,2,1,0:T(2,128)(2,1)S(1)}, u32[]{:S(2)}, u32[]{:S(2)}) collective-permute-start(bf16[4,20,2,256]{3,2,1,0:T(2,128)(2,1)S(1)} %get-tuple-element.33), channel_id=1, source_target_pairs={{0,1},{1,2},{2,3},{3,4},{4,5},{5,6},{6,7},{7,8},{8,9},{9,10},{10,1... | collective-permute-start | bytes 245768 | tf_op jit(solution)/shard_map/ppermute | solution.py:15
  43.8 1.3 copy-start.2
  43.8 1.3 copy-start.12
where the time goes:
time: 188 us; the launch traced here: 187 us
  blocking collectives  137 us (73%)
  starting transfers between devices  16.8 us (9%)
  waiting for transfers between devices  13.6 us (7%)
  matrix products  10.4 us (6%)
  local copies, waits for them, and re-layouts  6.82 us (4%)
    psum x1, blocking collectives, per_device(): lax.psum((term_reduce, term_dilated, term_expand), ('lat', 'lon'))  137 us
    ppermute x4, starting transfers between devices, with_halo(): lax.ppermute(tail, axis, [(i, (i + 1) % count) for i in range(ends)])  11.1 us
    ppermute x4, waiting for transfers between devices, with_halo(): lax.ppermute(head, axis, [((i + 1) % count, i) for i in range(ends)])  8.44 us
    unnamed x45, local copies, waits for them, and re-layouts  6.35 us
    ppermute x4, starting transfers between devices, with_halo(): lax.ppermute(head, axis, [((i + 1) % count, i) for i in range(ends)])  5.67 us
    ppermute x4, waiting for transfers between devices, with_halo(): lax.ppermute(tail, axis, [(i, (i + 1) % count) for i in range(ends)])  5.2 us
    dot_general x3, matrix products, pixel_sum(): lax.dot_general(left, right, (((0,), (0,)), ((), ())), preferred_element_...  3.8 us
  transfers between devices with their start and end apart: 8, of which 6 were waited for; matrix products, arithmetic and copies ran while one was open for 2% of the time, Pallas kernels for 0%

commit v1 on v0

v1 whole, which is shorter than its diff:
```python
import functools
import math

import jax
import jax.numpy as jnp
from jax import lax
from jax.experimental import pallas as pl
from jax.experimental.pallas import tpu as pltpu
from jax.sharding import PartitionSpec as P

MESH = pl.DeviceIdType.MESH
F32, BF16 = jnp.float32, jnp.bfloat16


def smooth(pre):
    return pre * jax.nn.sigmoid(pre)


def slope(pre):
    sig = jax.nn.sigmoid(pre)
    return sig * (1.0 + pre * (1.0 - sig))


def dot(left, right):
    return jnp.dot(left, right, preferred_element_type=F32)


def dot_rt(left, right):
    return lax.dot_general(left, right, (((1,), (1,)), ((), ())), preferred_element_type=F32)


def dot_lt(left, right):
    return lax.dot_general(left, right, (((0,), (0,)), ((), ())), preferred_element_type=F32)


def up(n, m):
    return -(-n // m) * m


class Term:
    def __init__(self, rows_a, rows_b, ring, depth):
        self.ra, self.rb, self.rows = rows_a, rows_b, rows_a + rows_b
        self.start = (0, rows_a)
        self.part = (rows_a, rows_b)
        self.first = (rows_a // ring, rows_b // ring)
        self.second = (rows_a // ring**2, rows_b // ring**2)
        self.joined = sum(self.second)
        self.zrows = up(self.joined, 8 * depth) // depth

    def scratch(self, ring, depth):
        return [
            pltpu.VMEM((2, self.rows, 128), BF16),
            pltpu.VMEM((self.rows, 128), BF16),
            pltpu.VMEM((self.rows, 128), BF16),
            pltpu.VMEM((ring - 1, self.first[0], 128), BF16),
            pltpu.VMEM((ring - 1, self.first[1], 128), BF16),
            pltpu.VMEM((self.first[0], 128), BF16),
            pltpu.VMEM((self.first[1], 128), BF16),
            pltpu.VMEM((ring - 1, self.second[0], 128), BF16),
            pltpu.VMEM((ring - 1, self.second[1], 128), BF16),
            pltpu.VMEM((depth * self.zrows, 128), F32),
            pltpu.VMEM((depth - 1, self.zrows, 128), F32),
            pltpu.VMEM((self.zrows, 128), F32),
            pltpu.VMEM((depth * self.zrows, 128), F32),
            pltpu.VMEM((2, self.rows, 128), BF16),
        ]


def kernel(ring, depth, terms, dims, *refs):
    batch, height, width, chan_in, chan_mid = dims
    pixels = batch * height * width
    h2n, w2n = height // 2, width // 2
    lon_n = ring * ring * 2
    (x_hbm, wr_hbm, wd_hbm, we_hbm, go_hbm, gr, br, gd, bd, ge, be, pw,
     gi_hbm, gred_hbm, gdil_hbm, gexp_hbm,
     x_v, wr_v, wd_v, we_v, go_v, perm, back, pre_one, slope_two, gfull, gthree, p_one, p_two, gi_v,
     *rest) = refs
    n_bufs = 14
    bufs = [rest[n_bufs * i : n_bufs * (i + 1)] for i in range(3)]
    load_sem, store_sem, send_sem, recv_sem = rest[3 * n_bufs :]

    lat, lon = lax.axis_index("lat"), lax.axis_index("lon")
    core, plane = lon % 2, lon // 2
    gx, gy = plane // ring, plane % ring

    loads = [
        pltpu.make_async_copy(src, dst, load_sem.at[i])
        for i, (src, dst) in enumerate(
            [(x_hbm, x_v), (wr_hbm, wr_v), (wd_hbm, wd_v), (we_hbm, we_v), (go_hbm, go_v)]
        )
    ]
    for load in loads:
        load.start()

    def at_xy(ax, ay):
        return (lat, (ax * ring + ay) * 2 + core)

    barrier = pltpu.get_barrier_semaphore()
    greet = [(lat, lon + 1 - 2 * core)]
    greet += [at_xy((gx + s) % ring, gy) for s in range(1, ring)]
    greet += [at_xy(gx, (gy + s) % ring) for s in range(1, ring)]
    greet += [((lat + s) % depth, lon) for s in range(1, depth)]
    for dl in (-1, 0, 1):
        for dw in (-1, 1):
            greet.append(((lat + dl + depth) % depth, (lon + dw + lon_n) % lon_n))
    for device in greet:
        pl.semaphore_signal(barrier, inc=1, device_id=device, device_id_type=MESH)

    def natural(p):
        return (
            ((p // 4) % batch) * (height * width)
            + (2 * (p // (16 * w2n)) + (p // 2) % 2) * width
            + 2 * ((p // 16) % w2n)
            + p % 2
        )

    lanes = lax.broadcasted_iota(jnp.int32, (pixels, 128), 1)
    rows = lax.broadcasted_iota(jnp.int32, (pixels, 128), 0)
    source = natural(lax.broadcasted_iota(jnp.int32, (pixels, 1), 0))
    for j in range(pixels // 128):
        cols = slice(j * 128, (j + 1) * 128)
        perm[:, cols] = jnp.where(source == lanes + j * 128, 1.0, 0.0).astype(BF16)
        target = natural(lax.broadcasted_iota(jnp.int32, (1, 128), 1) + j * 128)
        back[:, cols] = jnp.where(target == rows, 1.0, 0.0).astype(BF16)

    copies = []

    def remote(src, dst, device):
        i = len(copies)
        copy = pltpu.make_async_remote_copy(
            src_ref=src,
            dst_ref=dst,
            send_sem=send_sem.at[i],
            recv_sem=recv_sem.at[i],
            device_id=device,
            device_id_type=MESH,
        )
        copies.append(copy)
        return copy

    def send(src, dst, device):
        copy = remote(src, dst, device)
        copy.start()
        return copy

    guarded = []

    def halo(p_ref):
        hi, wi = slice(1, 1 + h2n), slice(1, 1 + w2n)

        @pl.when(lat == 0)
        def _():
            p_ref[0] = jnp.zeros_like(p_ref[0])

        @pl.when(lat == depth - 1)
        def _():
            p_ref[h2n + 1] = jnp.zeros_like(p_ref[h2n + 1])

        west, east = (lon + lon_n - 1) % lon_n, (lon + 1) % lon_n
        plan = []
        for dl in (0, -1, 1):
            row_src = {0: hi, -1: 1, 1: h2n}[dl]
            row_dst = {0: hi, -1: h2n + 1, 1: 0}[dl]
            there = (lat + dl + depth) % depth
            for dw in (0, -1, 1):
                if dl == 0 and dw == 0:
                    continue
                col_src = {0: wi, -1: 1, 1: w2n}[dw]
                col_dst = {0: wi, -1: w2n + 1, 1: 0}[dw]
                device = (there, {0: lon, -1: west, 1: east}[dw])
                copy = remote(p_ref.at[row_src, col_src], p_ref.at[row_dst, col_dst], device)
                plan.append((dl, copy))

        def sends(copy):
            return copy.start

        def on(dl, receiving, action):
            if dl == 0:
                action()
                return
            toward_low = (dl == -1) != receiving
            pl.when(lat > 0 if toward_low else lat < depth - 1)(action)

        for dl, copy in plan:
            on(dl, False, copy.start)
        guarded.extend((dl, copy, on) for dl, copy in plan)

        def wait():
            for dl, copy in plan:
                on(dl, True, copy.wait_recv)

        return wait

    def tap(p_ref, row, col):
        return p_ref[row : row + h2n, col : col + w2n].reshape(pixels, chan_mid)

    def to_natural(value):
        high = value.astype(BF16)
        low = (value - high.astype(F32)).astype(BF16)
        return dot(back[...], high) + dot(back[...], low)

    sibling = (lat, lon + 1 - 2 * core)

    def put_term(t, first_row, value):
        own = bufs[t][0]
        n = value.shape[0]
        own[0, first_row : first_row + n] = value[:, :128].astype(BF16)
        own[1, first_row : first_row + n] = value[:, 128:].astype(BF16)

    def core_send(t, part):
        term, b = terms[t], bufs[t]
        span = slice(term.start[part], term.start[part] + term.part[part])
        return send(b[0].at[1 - core, span], b[1].at[span], sibling)

    def ring_pos(part, step):
        return (gx, gy)[part ^ step]

    def ring_dev(part, step, s):
        if part ^ step == 0:
            return at_xy((gx + s) % ring, gy)
        return at_xy(gx, (gy + s) % ring)

    def pair_and_first(t, part, arrived):
        term, b = terms[t], bufs[t]
        arrived.wait_recv()
        lo, n = term.start[part], term.part[part]
        span = slice(lo, lo + n)
        b[2][span] = (b[0][core, span].astype(F32) + b[1][span].astype(F32)).astype(BF16)
        step = term.first[part]
        out = []
        for s in range(1, ring):
            peer = (ring_pos(part, 0) + s) % ring
            src = b[2].at[pl.ds(pl.multiple_of(lo + peer * step, 16), step)]
            out.append(send(src, b[3 + part].at[s - 1], ring_dev(part, 0, s)))
        return out

    def second(t, part, arrived):
        term, b = terms[t], bufs[t]
        for copy in arrived:
            copy.wait_recv()
        lo, n = term.start[part], term.first[part]
        mine = pl.ds(pl.multiple_of(lo + ring_pos(part, 0) * n, 16), n)
        total = b[2][mine].astype(F32)
        for s in range(ring - 1):
            total = total + b[3 + part][s].astype(F32)
        b[5 + part][...] = total.astype(BF16)
        step = term.second[part]
        out = []
        for s in range(1, ring):
            peer = (ring_pos(part, 1) + s) % ring
            src = b[5 + part].at[pl.ds(pl.multiple_of(peer * step, 16), step)]
            out.append(send(src, b[7 + part].at[s - 1], ring_dev(part, 1, s)))
        return out

    def third(t, arrived):
        term, b = terms[t], bufs[t]
        at = 0
        for part in (0, 1):
            for copy in arrived[part]:
                copy.wait_recv()
            n = term.second[part]
            mine = pl.ds(pl.multiple_of(ring_pos(part, 1) * n, 16), n)
            total = b[5 + part][mine].astype(F32)
            for s in range(ring - 1):
                total = total + b[7 + part][s].astype(F32)
            b[9][at : at + n] = total
            at += n
        if at < depth * term.zrows:
            b[9][at:] = jnp.zeros((depth * term.zrows - at, 128), F32)
        out = []
        for s in range(1, depth):
            peer = (lat + s) % depth
            src = b[9].at[pl.ds(pl.multiple_of(peer * term.zrows, 8), term.zrows)]
            out.append(send(src, b[10].at[s - 1], (peer, lon)))
        return out

    def fourth(t, arrived):
        term, b = terms[t], bufs[t]
        for copy in arrived:
            copy.wait_recv()
        mine = pl.ds(pl.multiple_of(lat * term.zrows, 8), term.zrows)
        total = b[9][mine]
        for s in range(depth - 1):
            total = total + b[10][s]
        b[11][...] = total
        b[12][mine] = total
        return [
            send(b[11], b[12].at[mine], ((lat + s) % depth, lon)) for s in range(1, depth)
        ]

    def fifth(t, arrived):
        term, b = terms[t], bufs[t]
        for copy in arrived:
            copy.wait_recv()
        at, outs = 0, []
        for part in (0, 1):
            n = term.second[part]
            place = term.start[part] + ring_pos(part, 0) * term.first[part] + ring_pos(part, 1) * n
            here = pl.ds(pl.multiple_of(place, 16), n)
            b[13][core, here] = b[12][at : at + n].astype(BF16)
            at += n
            block = b[13].at[core, here]
            outs.append([send(block, block, ring_dev(part, 1, s)) for s in range(1, ring)])
        return outs

    def sixth(t, arrived):
        term, b = terms[t], bufs[t]
        outs = []
        for part in (0, 1):
            for copy in arrived[part]:
                copy.wait_recv()
            n = term.first[part]
            place = term.start[part] + ring_pos(part, 0) * n
            block = b[13].at[core, pl.ds(pl.multiple_of(place, 16), n)]
            outs.append([send(block, block, ring_dev(part, 0, s)) for s in range(1, ring)])
        return outs

    def seventh(t, arrived):
        b = bufs[t]
        for part in (0, 1):
            for copy in arrived[part]:
                copy.wait_recv()
        return send(b[13].at[core], b[13].at[core], sibling)

    stores = []

    def store(src, dst):
        copy = pltpu.make_async_copy(src, dst, store_sem.at[len(stores)])
        copy.start()
        stores.append(copy)

    loads[0].wait()
    loads[1].wait()
    pre_one[...] = dot(x_v[...], wr_v[...]) * gr[...] + br[...]
    mid_one = smooth(pre_one[...]).astype(BF16)
    hi, wi = slice(1, 1 + h2n), slice(1, 1 + w2n)
    p_one[hi, wi] = dot(perm[...], mid_one).astype(BF16).reshape(h2n, w2n, 16, chan_mid)
    pl.semaphore_wait(barrier, len(greet))
    wait_one = halo(p_one)
    for load in loads[2:]:
        load.wait()
    total = dot(tap(p_one, 1, 1), wd_v[4])
    wait_one()
    for i in (0, 1, 2, 3, 5, 6, 7, 8):
        total = total + dot(tap(p_one, i // 3, i % 3), wd_v[i])
    pre_two = to_natural(total * gd[...] + bd[...])
    mid_two = smooth(pre_two).astype(BF16)
    slope_two[...] = slope(pre_two) * gd[...]

    blocks = chan_in // 256
    total = None
    for j in range(blocks):
        cols = slice(j * 256, (j + 1) * 256)
        w_block = we_v[:, cols]
        pre_three = dot(mid_two, w_block) * ge[:, cols] + be[:, cols] + x_v[:, cols].astype(F32)
        full = go_v[:, cols].astype(F32) * pw[...] * slope(pre_three)
        gfull[:, cols] = full
        grad_three = (full * ge[:, cols]).astype(BF16)
        gthree[:, cols] = grad_three
        term = dot_rt(grad_three, w_block)
        total = term if total is None else total + term
    grad_two = (total * slope_two[...]).astype(BF16)
    p_two[hi, wi] = dot(perm[...], grad_two).astype(BF16).reshape(h2n, w2n, 16, chan_mid)
    wait_two = halo(p_two)

    for j in range(blocks):
        put_term(0, j * 256, dot_lt(mid_two, gthree[:, j * 256 : (j + 1) * 256]))
    e_core = [core_send(0, 0), core_send(0, 1)]
    center = tap(p_two, 1, 1)
    taps_a = terms[1].ra // chan_mid
    d_core = []
    for i in range(9):
        put_term(1, i * chan_mid, dot_lt(tap(p_one, i // 3, i % 3), center))
        if i == taps_a - 1:
            d_core.append(core_send(1, 0))
    d_core.append(core_send(1, 1))
    e_first = [pair_and_first(0, part, e_core[part]) for part in (0, 1)]

    total = dot_rt(center, wd_v[4])
    wait_two()
    for i in (0, 1, 2, 3, 5, 6, 7, 8):
        total = total + dot_rt(tap(p_two, 2 - i // 3, 2 - i % 3), wd_v[i])
    grad_one = (to_natural(total) * slope(pre_one[...]) * gr[...]).astype(BF16)
    r_core = []
    for j in range(2):
        half = chan_in // 2
        put_term(2, j * half, dot_lt(x_v[:, j * half : (j + 1) * half], grad_one))
        r_core.append(core_send(2, j))
    d_first = [pair_and_first(1, part, d_core[part]) for part in (0, 1)]
    e_second = [second(0, part, e_first[part]) for part in (0, 1)]
    for j in range(blocks):
        cols = slice(j * 256, (j + 1) * 256)
        gi_v[:, cols] = (dot_rt(grad_one, wr_v[cols, :]) + gfull[:, cols]).astype(BF16)
    store(gi_v, gi_hbm)
    r_first = [pair_and_first(2, part, r_core[part]) for part in (0, 1)]
    e_third = third(0, e_second)
    d_second = [second(1, part, d_first[part]) for part in (0, 1)]
    r_second = [second(2, part, r_first[part]) for part in (0, 1)]
    d_third = third(1, d_second)
    e_fourth = fourth(0, e_third)
    r_third = third(2, r_second)
    d_fourth = fourth(1, d_third)
    e_fifth = fifth(0, e_fourth)
    r_fourth = fourth(2, r_third)
    d_fifth = fifth(1, d_fourth)
    e_sixth = sixth(0, e_fifth)
    r_fifth = fifth(2, r_fourth)
    d_sixth = sixth(1, d_fifth)
    e_last = seventh(0, e_sixth)
    r_sixth = sixth(2, r_fifth)
    d_last = seventh(1, d_sixth)
    r_last = seventh(2, r_sixth)

    e_last.wait_recv()
    for side in (0, 1):
        for j in range(blocks):
            first = j * 256 + side * 128
            store(
                bufs[0][13].at[side, j * 256 : (j + 1) * 256], gexp_hbm.at[:, first : first + 128]
            )
    d_last.wait_recv()
    for side in (0, 1):
        store(bufs[1][13].at[side], gdil_hbm.at[:, side * 128 : (side + 1) * 128])
    r_last.wait_recv()
    for side in (0, 1):
        store(bufs[2][13].at[side], gred_hbm.at[:, side * 128 : (side + 1) * 128])
    halo_copies = {id(copy) for _, copy, _ in guarded}
    for dl, copy, on in guarded:
        on(dl, False, copy.wait_send)
    for copy in copies:
        if id(copy) not in halo_copies:
            copy.wait_send()
    for copy in stores:
        copy.wait()


def per_device(
    ring,
    depth,
    inputs,
    w_reduce,
    gain_reduce,
    bias_reduce,
    w_dilated,
    gain_dilated,
    bias_dilated,
    w_expand,
    gain_expand,
    bias_expand,
    grad_out,
    labels,
    class_weight,
):
    batch, height, width, chan_in = inputs.shape
    chan_mid = w_reduce.shape[1]
    pixels = batch * height * width
    classes = jnp.arange(class_weight.shape[0], dtype=jnp.int32)
    weight = jnp.sum(
        jnp.where(labels.reshape(pixels, 1) == classes, class_weight, 0.0), axis=-1, keepdims=True
    )
    half = chan_in // 2
    terms = [
        Term(half, half, ring, depth),
        Term(5 * chan_mid, 4 * chan_mid, ring, depth),
        Term(half, half, ring, depth),
    ]
    scratch = [
        pltpu.VMEM((pixels, chan_in), BF16),
        pltpu.VMEM((chan_in, chan_mid), BF16),
        pltpu.VMEM((9, chan_mid, chan_mid), BF16),
        pltpu.VMEM((chan_mid, chan_in), BF16),
        pltpu.VMEM((pixels, chan_in), BF16),
        pltpu.VMEM((pixels, pixels), BF16),
        pltpu.VMEM((pixels, pixels), BF16),
        pltpu.VMEM((pixels, chan_mid), F32),
        pltpu.VMEM((pixels, chan_mid), F32),
        pltpu.VMEM((pixels, chan_in), F32),
        pltpu.VMEM((pixels, chan_in), BF16),
        pltpu.VMEM((height // 2 + 2, width // 2 + 2, 16, chan_mid), BF16),
        pltpu.VMEM((height // 2 + 2, width // 2 + 2, 16, chan_mid), BF16),
        pltpu.VMEM((pixels, chan_in), BF16),
    ]
    for term in terms:
        scratch += term.scratch(ring, depth)
    per_term = 2 + 12 * (ring - 1) // 3 * 2 + 2 * (depth - 1) + 1
    n_remote = 16 + 3 * (2 + 8 * (ring - 1) + 2 * (depth - 1) + 1)
    scratch += [
        pltpu.SemaphoreType.DMA((5,)),
        pltpu.SemaphoreType.DMA((2 * (chan_in // 256) + 5,)),
        pltpu.SemaphoreType.DMA((n_remote,)),
        pltpu.SemaphoreType.DMA((n_remote,)),
    ]
    anywhere = pl.BlockSpec(memory_space=pl.ANY)
    vmem = pl.BlockSpec(memory_space=pltpu.VMEM)
    grad_inputs, grad_reduce, grad_dilated, grad_expand = pl.pallas_call(
        functools.partial(
            kernel, ring, depth, terms, (batch, height, width, chan_in, chan_mid)
        ),
        out_shape=(
            jax.ShapeDtypeStruct((pixels, chan_in), BF16),
            jax.ShapeDtypeStruct((chan_in, chan_mid), BF16),
            jax.ShapeDtypeStruct((9 * chan_mid, chan_mid), BF16),
            jax.ShapeDtypeStruct((chan_mid, chan_in), BF16),
        ),
        in_specs=[anywhere] * 5 + [vmem] * 7,
        out_specs=(anywhere,) * 4,
        scratch_shapes=scratch,
        compiler_params=pltpu.CompilerParams(
            collective_id=0, has_side_effects=True, vmem_limit_bytes=60 * 2**20
        ),
    )(
        inputs.reshape(pixels, chan_in),
        w_reduce,
        w_dilated.reshape(9, chan_mid, chan_mid),
        w_expand,
        grad_out.reshape(pixels, chan_in),
        gain_reduce.reshape(1, -1),
        bias_reduce.reshape(1, -1),
        gain_dilated.reshape(1, -1),
        bias_dilated.reshape(1, -1),
        gain_expand.reshape(1, -1),
        bias_expand.reshape(1, -1),
        weight,
    )
    return (
        grad_inputs.reshape(batch, height, width, chan_in),
        grad_reduce,
        grad_dilated.reshape(3, 3, chan_mid, chan_mid),
        grad_expand,
    )


def solution(mesh):
    ring = math.isqrt(mesh.shape["lon"] // 2)
    field = P(None, "lat", "lon", None)
    return jax.shard_map(
        functools.partial(per_device, ring, mesh.shape["lat"]),
        mesh=mesh,
        in_specs=(field,) + (P(),) * 9 + (field, P(None, "lat", "lon"), P()),
        out_specs=(field, P(), P(), P()),
        check_vma=False,
    )
```

time: 188 us -> 72.5 us (0.39)
  blocking collectives: 137 us -> 0 us
  Pallas kernels: 0 us -> 63.7 us
  starting transfers between devices: 16.8 us -> 0 us
  waiting for transfers between devices: 13.6 us -> 0 us
  matrix products: 10.4 us -> 0 us
    psum x1 -> x0, blocking collectives: 137 us -> none  [per_device(): lax.psum((term_reduce, term_dilated, term_expand), ('lat', 'lon'))]
    pallas_call x0 -> x1, Pallas kernels: none -> 63.7 us  [per_device(): pl.pallas_call(functools.partial(kernel, ring, depth, terms, (batch, heig...]
    ppermute x8 -> x0, starting transfers between devices: 16.8 us -> none  [the longest x4 11.1 us: with_halo(): lax.ppermute(tail, axis, [(i, (i + 1) % count) for i in range(ends)])]
    ppermute x8 -> x0, waiting for transfers between devices: 13.6 us -> none  [the longest x4 8.44 us: with_halo(): lax.ppermute(head, axis, [((i + 1) % count, i) for i in range(ends)])]
    dot_general x9 -> x0, matrix products: 10.4 us -> none  [the longest x3 3.8 us: pixel_sum(): lax.dot_general(left, right, (((0,), (0,)), ((), ())), preferred_element_...]
    unnamed x45 -> x11, local copies, waits for them, and re-layouts: 6.35 us -> 6.17 us
  transfers between devices with their start and end apart: 8 -> 0, of which waited for: 6 -> 0; matrix products, arithmetic and copies ran while one was open for 2% -> 0% of each run, Pallas kernels for 0% -> 0%
where the time goes in v1:
time: 72.5 us; the launch traced here: 72.3 us
  Pallas kernels  63.7 us (88%)
  local copies, waits for them, and re-layouts  7.12 us (10%)
  other arithmetic  0.74 us (1%)
    pallas_call x1, Pallas kernels, per_device(): pl.pallas_call(functools.partial(kernel, ring, depth, terms, (batch, heig...  63.7 us
    unnamed x11, local copies, waits for them, and re-layouts  6.17 us

profile of v1, /device:TPU:1, one launch (start us, length us, event | category | flops | bytes accessed | tf_op | source)
XLA Modules:
  0.0 72.3 jit_solution(10683516743816611173)
XLA Ops:
  0.6 0.8 %copy.19 = s32[4,16,8]{2,1,0:T(8,128)S(1)} copy(s32[4,16,8]{1,2,0:T(8,128)} %param.24) | data formatting | bytes 4096 | tf_op args[11]
  1.4 0.1 eq.15
  1.5 0.7 %select_reduce_fusion = f32[512]{0:T(512)S(1)} fusion(f32[3]{0:T(128)} %param.25, s32[512]{0:T(512)S(1)} %eq.15), kind=kLoop, calls=%fused_computation | loop fusion | flops 4096 | bytes 4108 | tf_op jit(solution)/shard_map/reduce_sum | solution.py:458
  2.3 0.9 %copy.20.refs_11_ = f32[512,1]{1,0:T(8,128)} copy(f32[512,1]{0,1:T(1,128)S(1)} %bitcast.17) | data formatting | bytes 4096 | tf_op jit(solution)/shard_map/broadcast_in_dim | solution.py:458
  3.1 63.7 %shard_map.156 = (bf16[512,1024]{1,0:T(8,128)(2,1)}, bf16[1024,256]{1,0:T(8,128)(2,1)}, bf16[2304,256]{1,0:T(8,128)(2,1)}, bf16[256,1024]{1,0:T(8,128)(2,1)}) custom-call(bf16[512,1024]{1,0:T(8,128)(2,1)} %bitcast.15, bf16[1024,256]{1,0:T(8,128)(2,1)} %refs_1_.1, bf16[9,256,256]{2,1,0:T(8,128)(2,1)} %bitcast.13, bf16[256,1024]{1,0:T(8,128)(2,1)} %refs_3_.1, ...), custom_call_target="tpu_custom_call" | custom-call | tf_op jit(solution)/shard_map/pallas_call | solution.py:495
  66.9 0.0 copy-start.2
  66.9 0.0 copy-start
  66.9 2.4 %copy.25 = bf16[4,16,8,1024]{3,2,1,0:T(8,128)(2,1)} copy(bf16[4,16,8,1024]{3,2,1,0:T(8,128)(2,1)} %bitcast.14) | data formatting | bytes 2097152
  69.3 0.0 copy-done.2
  69.3 0.8 %copy.26 = bf16[1024,256]{1,0:T(8,128)(2,1)} copy(bf16[1024,256]{1,0:T(8,128)(2,1)S(1)} %copy-done.2) | data formatting | bytes 1048576
  70.1 0.0 copy-done
  70.1 0.0 copy-start.1
  70.1 1.0 %copy.27 = bf16[3,3,256,256]{3,2,1,0:T(8,128)(2,1)} copy(bf16[3,3,256,256]{3,2,1,0:T(8,128)(2,1)S(1)} %bitcast.12) | data formatting | bytes 2359296
  71.1 0.4 copy-done.1
  71.5 0.8 %copy.28 = bf16[256,1024]{1,0:T(8,128)(2,1)} copy(bf16[256,1024]{1,0:T(8,128)(2,1)S(1)} %copy-done.1) | data formatting | bytes 1048576
Async XLA Ops:
  66.9 2.4 %copy-start.2 = (bf16[1024,256]{1,0:T(8,128)(2,1)S(1)}, bf16[1024,256]{1,0:T(8,128)(2,1)}, u32[]{:S(2)}) copy-start(bf16[1024,256]{1,0:T(8,128)(2,1)} %get-tuple-element.17) | copy-start | bytes 1572868
  66.9 3.2 %copy-start = (bf16[2304,256]{1,0:T(8,128)(2,1)S(1)}, bf16[2304,256]{1,0:T(8,128)(2,1)}, u32[]{:S(2)}) copy-start(bf16[2304,256]{1,0:T(8,128)(2,1)} %get-tuple-element.10) | copy-start | bytes 3538948
  70.1 1.4 %copy-start.1 = (bf16[256,1024]{1,0:T(8,128)(2,1)S(1)}, bf16[256,1024]{1,0:T(8,128)(2,1)}, u32[]{:S(2)}) copy-start(bf16[256,1024]{1,0:T(8,128)(2,1)} %get-tuple-element.19) | copy-start | bytes 1572868

commit v2 on v1

--- a/solution.py
+++ b/solution.py
@@ -59,10 +59,11 @@
             pltpu.VMEM((ring - 1, self.second[0], 128), BF16),
             pltpu.VMEM((ring - 1, self.second[1], 128), BF16),
             pltpu.VMEM((depth * self.zrows, 128), F32),
-            pltpu.VMEM((depth - 1, self.zrows, 128), F32),
-            pltpu.VMEM((self.zrows, 128), F32),
-            pltpu.VMEM((depth * self.zrows, 128), F32),
+            pltpu.VMEM((depth - 1, self.zrows, 128), BF16),
+            pltpu.VMEM((self.zrows, 128), BF16),
+            pltpu.VMEM((depth, self.zrows, 128), BF16),
             pltpu.VMEM((2, self.rows, 128), BF16),
+            pltpu.VMEM((depth, self.zrows, 128), BF16),
         ]
 
 
@@ -71,11 +72,13 @@
     pixels = batch * height * width
     h2n, w2n = height // 2, width // 2
     lon_n = ring * ring * 2
-    (x_hbm, wr_hbm, wd_hbm, we_hbm, go_hbm, gr, br, gd, bd, ge, be, pw,
+    (x_hbm, wr_hbm, gr_hbm, br_hbm, wd_hbm, gd_hbm, bd_hbm, we_hbm, ge_hbm, be_hbm, go_hbm,
+     label_hbm, class_weight,
      gi_hbm, gred_hbm, gdil_hbm, gexp_hbm,
-     x_v, wr_v, wd_v, we_v, go_v, perm, back, pre_one, slope_two, gfull, gthree, p_one, p_two, gi_v,
+     x_v, wr_v, gr, br, wd_v, gd, bd, we_v, ge, be, go_v, label_v,
+     pw, perm, back, pre_one, slope_two, gfull, gthree, p_one, p_two, gi_v,
      *rest) = refs
-    n_bufs = 14
+    n_bufs = 15
     bufs = [rest[n_bufs * i : n_bufs * (i + 1)] for i in range(3)]
     load_sem, store_sem, send_sem, recv_sem = rest[3 * n_bufs :]
 
@@ -86,7 +89,11 @@
     loads = [
         pltpu.make_async_copy(src, dst, load_sem.at[i])
         for i, (src, dst) in enumerate(
-            [(x_hbm, x_v), (wr_hbm, wr_v), (wd_hbm, wd_v), (we_hbm, we_v), (go_hbm, go_v)]
+            [
+                (x_hbm, x_v), (wr_hbm, wr_v), (gr_hbm, gr), (br_hbm, br),
+                (label_hbm, label_v), (wd_hbm, wd_v), (gd_hbm, gd), (bd_hbm, bd),
+                (we_hbm, we_v), (ge_hbm, ge), (be_hbm, be), (go_hbm, go_v),
+            ]
         )
     ]
     for load in loads:
@@ -267,11 +274,11 @@
             at += n
         if at < depth * term.zrows:
             b[9][at:] = jnp.zeros((depth * term.zrows - at, 128), F32)
+        b[14][...] = b[9][...].reshape(depth, term.zrows, 128).astype(BF16)
         out = []
         for s in range(1, depth):
             peer = (lat + s) % depth
-            src = b[9].at[pl.ds(pl.multiple_of(peer * term.zrows, 8), term.zrows)]
-            out.append(send(src, b[10].at[s - 1], (peer, lon)))
+            out.append(send(b[14].at[peer], b[10].at[s - 1], (peer, lon)))
         return out
 
     def fourth(t, arrived):
@@ -281,11 +288,11 @@
         mine = pl.ds(pl.multiple_of(lat * term.zrows, 8), term.zrows)
         total = b[9][mine]
         for s in range(depth - 1):
-            total = total + b[10][s]
-        b[11][...] = total
-        b[12][mine] = total
+            total = total + b[10][s].astype(F32)
+        b[11][...] = total.astype(BF16)
+        b[12][lat] = total.astype(BF16)
         return [
-            send(b[11], b[12].at[mine], ((lat + s) % depth, lon)) for s in range(1, depth)
+            send(b[11], b[12].at[lat], ((lat + s) % depth, lon)) for s in range(1, depth)
         ]
 
     def fifth(t, arrived):
@@ -293,11 +300,12 @@
         for copy in arrived:
             copy.wait_recv()
         at, outs = 0, []
+        whole = b[12][...].astype(F32).reshape(depth * term.zrows, 128)
         for part in (0, 1):
             n = term.second[part]
             place = term.start[part] + ring_pos(part, 0) * term.first[part] + ring_pos(part, 1) * n
             here = pl.ds(pl.multiple_of(place, 16), n)
-            b[13][core, here] = b[12][at : at + n].astype(BF16)
+            b[13][core, here] = whole[at : at + n].astype(BF16)
             at += n
             block = b[13].at[core, here]
             outs.append([send(block, block, ring_dev(part, 1, s)) for s in range(1, ring)])
@@ -329,16 +337,30 @@
         copy.start()
         stores.append(copy)
 
-    loads[0].wait()
-    loads[1].wait()
+    for load in loads[:4]:
+        load.wait()
     pre_one[...] = dot(x_v[...], wr_v[...]) * gr[...] + br[...]
     mid_one = smooth(pre_one[...]).astype(BF16)
     hi, wi = slice(1, 1 + h2n), slice(1, 1 + w2n)
     p_one[hi, wi] = dot(perm[...], mid_one).astype(BF16).reshape(h2n, w2n, 16, chan_mid)
     pl.semaphore_wait(barrier, len(greet))
     wait_one = halo(p_one)
-    for load in loads[2:]:
+    for load in loads[4:]:
         load.wait()
+    lab_rows = batch * width
+    pixel = lax.broadcasted_iota(jnp.int32, (pixels, lab_rows), 0)
+    row = (pixel // (height * width)) * width + pixel % width
+    row_hot = jnp.where(
+        row == lax.broadcasted_iota(jnp.int32, (pixels, lab_rows), 1), 1.0, 0.0
+    ).astype(BF16)
+    picked = dot(row_hot, label_v[...].astype(F32).astype(BF16))
+    pixel = lax.broadcasted_iota(jnp.int32, (pixels, height), 0)
+    lane_hot = (pixel // width) % height == lax.broadcasted_iota(jnp.int32, (pixels, height), 1)
+    label = jnp.sum(jnp.where(lane_hot, picked, 0.0), axis=1, keepdims=True)
+    weight = class_weight[0, 0]
+    for k in range(1, class_weight.shape[1]):
+        weight = jnp.where(label > k - 0.5, class_weight[0, k], weight)
+    pw[...] = jnp.broadcast_to(weight, pw.shape)
     total = dot(tap(p_one, 1, 1), wd_v[4])
     wait_one()
     for i in (0, 1, 2, 3, 5, 6, 7, 8):
@@ -373,8 +395,8 @@
         put_term(1, i * chan_mid, dot_lt(tap(p_one, i // 3, i % 3), center))
         if i == taps_a - 1:
             d_core.append(core_send(1, 0))
+            e_first = [pair_and_first(0, part, e_core[part]) for part in (0, 1)]
     d_core.append(core_send(1, 1))
-    e_first = [pair_and_first(0, part, e_core[part]) for part in (0, 1)]
 
     total = dot_rt(center, wd_v[4])
     wait_two()
@@ -454,10 +476,6 @@
     batch, height, width, chan_in = inputs.shape
     chan_mid = w_reduce.shape[1]
     pixels = batch * height * width
-    classes = jnp.arange(class_weight.shape[0], dtype=jnp.int32)
-    weight = jnp.sum(
-        jnp.where(labels.reshape(pixels, 1) == classes, class_weight, 0.0), axis=-1, keepdims=True
-    )
     half = chan_in // 2
     terms = [
         Term(half, half, ring, depth),
@@ -467,9 +485,17 @@
     scratch = [
         pltpu.VMEM((pixels, chan_in), BF16),
         pltpu.VMEM((chan_in, chan_mid), BF16),
+        pltpu.VMEM((1, chan_mid), F32),
+        pltpu.VMEM((1, chan_mid), F32),
         pltpu.VMEM((9, chan_mid, chan_mid), BF16),
+        pltpu.VMEM((1, chan_mid), F32),
+        pltpu.VMEM((1, chan_mid), F32),
         pltpu.VMEM((chan_mid, chan_in), BF16),
+        pltpu.VMEM((1, chan_in), F32),
+        pltpu.VMEM((1, chan_in), F32),
         pltpu.VMEM((pixels, chan_in), BF16),
+        pltpu.VMEM((batch * width, height), jnp.int32),
+        pltpu.VMEM((pixels, 1), F32),
         pltpu.VMEM((pixels, pixels), BF16),
         pltpu.VMEM((pixels, pixels), BF16),
         pltpu.VMEM((pixels, chan_mid), F32),
@@ -482,16 +508,15 @@
     ]
     for term in terms:
         scratch += term.scratch(ring, depth)
-    per_term = 2 + 12 * (ring - 1) // 3 * 2 + 2 * (depth - 1) + 1
     n_remote = 16 + 3 * (2 + 8 * (ring - 1) + 2 * (depth - 1) + 1)
     scratch += [
-        pltpu.SemaphoreType.DMA((5,)),
+        pltpu.SemaphoreType.DMA((12,)),
         pltpu.SemaphoreType.DMA((2 * (chan_in // 256) + 5,)),
         pltpu.SemaphoreType.DMA((n_remote,)),
         pltpu.SemaphoreType.DMA((n_remote,)),
     ]
     anywhere = pl.BlockSpec(memory_space=pl.ANY)
-    vmem = pl.BlockSpec(memory_space=pltpu.VMEM)
+    smem = pl.BlockSpec(memory_space=pltpu.SMEM)
     grad_inputs, grad_reduce, grad_dilated, grad_expand = pl.pallas_call(
         functools.partial(
             kernel, ring, depth, terms, (batch, height, width, chan_in, chan_mid)
@@ -502,7 +527,7 @@
             jax.ShapeDtypeStruct((9 * chan_mid, chan_mid), BF16),
             jax.ShapeDtypeStruct((chan_mid, chan_in), BF16),
         ),
-        in_specs=[anywhere] * 5 + [vmem] * 7,
+        in_specs=[anywhere] * 12 + [smem],
         out_specs=(anywhere,) * 4,
         scratch_shapes=scratch,
         compiler_params=pltpu.CompilerParams(
@@ -511,16 +536,17 @@
     )(
         inputs.reshape(pixels, chan_in),
         w_reduce,
-        w_dilated.reshape(9, chan_mid, chan_mid),
-        w_expand,
-        grad_out.reshape(pixels, chan_in),
         gain_reduce.reshape(1, -1),
         bias_reduce.reshape(1, -1),
+        w_dilated.reshape(9, chan_mid, chan_mid),
         gain_dilated.reshape(1, -1),
         bias_dilated.reshape(1, -1),
+        w_expand,
         gain_expand.reshape(1, -1),
         bias_expand.reshape(1, -1),
-        weight,
+        grad_out.reshape(pixels, chan_in),
+        labels.transpose(0, 2, 1).reshape(batch * width, height),
+        class_weight.reshape(1, -1),
     )
     return (
         grad_inputs.reshape(batch, height, width, chan_in),

time: 72.5 us -> 68.9 us (0.950)
  local copies, waits for them, and re-layouts: 7.12 us -> 5.38 us
  Pallas kernels: 63.7 us -> 62.7 us
  other arithmetic: 0.74 us -> 0 us
    pallas_call x1, Pallas kernels: 63.7 us -> 62.7 us  [per_device(): pl.pallas_call(functools.partial(kernel, ring, depth, terms, (batch, heig...]
    broadcast_in_dim x1 -> x0, local copies, waits for them, and re-layouts: 0.86 us -> none  [per_device(): jnp.sum(jnp.where(labels.reshape(pixels, 1) == classes, class_weight, 0.0...]
    unnamed x11 -> x10, local copies, waits for them, and re-layouts: 6.17 us -> 5.38 us
    reduce_sum x1 -> x0, other arithmetic: 0.74 us -> none  [per_device(): jnp.sum(jnp.where(labels.reshape(pixels, 1) == classes, class_weight, 0.0...]
where the time goes in v2:
time: 68.9 us; the launch traced here: 68.7 us
  Pallas kernels  62.7 us (91%)
  local copies, waits for them, and re-layouts  5.38 us (8%)
    pallas_call x1, Pallas kernels, per_device(): pl.pallas_call(functools.partial(kernel, ring, depth, terms, (batch, heig...  62.7 us
    unnamed x10, local copies, waits for them, and re-layouts  5.38 us

profile of v2, /device:TPU:1, one launch (start us, length us, event | category | flops | bytes accessed | tf_op | source)
XLA Modules:
  0.0 68.7 jit_solution(321784444326567177)
XLA Ops:
  0.6 62.7 %shard_map.156 = (bf16[512,1024]{1,0:T(8,128)(2,1)}, bf16[1024,256]{1,0:T(8,128)(2,1)}, bf16[2304,256]{1,0:T(8,128)(2,1)}, bf16[256,1024]{1,0:T(8,128)(2,1)}) custom-call(bf16[512,1024]{1,0:T(8,128)(2,1)} %bitcast.18, bf16[1024,256]{1,0:T(8,128)(2,1)} %refs_1_.1, f32[1,256]{1,0:T(1,128)} %bitcast.23, f32[1,256]{1,0:T(1,128)} %bitcast.24, ...), custom_call_target="tpu_custom_call" | custom-call | tf_op jit(solution)/shard_map/pallas_call | solution.py:520
  63.4 0.0 copy-start.2
  63.4 0.0 copy-start
  63.4 2.4 %copy.21 = bf16[4,16,8,1024]{3,2,1,0:T(8,128)(2,1)} copy(bf16[4,16,8,1024]{3,2,1,0:T(8,128)(2,1)} %bitcast.17) | data formatting | bytes 2097152
  65.8 0.0 copy-done.2
  65.8 0.8 %copy.22 = bf16[1024,256]{1,0:T(8,128)(2,1)} copy(bf16[1024,256]{1,0:T(8,128)(2,1)S(1)} %copy-done.2) | data formatting | bytes 1048576
  66.6 0.0 copy-done
  66.6 0.0 copy-start.1
  66.6 1.0 %copy.23 = bf16[3,3,256,256]{3,2,1,0:T(8,128)(2,1)} copy(bf16[3,3,256,256]{3,2,1,0:T(8,128)(2,1)S(1)} %bitcast.15) | data formatting | bytes 2359296
  67.6 0.4 copy-done.1
  68.0 0.8 %copy.24 = bf16[256,1024]{1,0:T(8,128)(2,1)} copy(bf16[256,1024]{1,0:T(8,128)(2,1)S(1)} %copy-done.1) | data formatting | bytes 1048576
Async XLA Ops:
  63.4 2.4 %copy-start.2 = (bf16[1024,256]{1,0:T(8,128)(2,1)S(1)}, bf16[1024,256]{1,0:T(8,128)(2,1)}, u32[]{:S(2)}) copy-start(bf16[1024,256]{1,0:T(8,128)(2,1)} %get-tuple-element.17) | copy-start | bytes 1572868
  63.4 3.2 %copy-start = (bf16[2304,256]{1,0:T(8,128)(2,1)S(1)}, bf16[2304,256]{1,0:T(8,128)(2,1)}, u32[]{:S(2)}) copy-start(bf16[2304,256]{1,0:T(8,128)(2,1)} %get-tuple-element.10) | copy-start | bytes 3538948
  66.6 1.4 %copy-start.1 = (bf16[256,1024]{1,0:T(8,128)(2,1)S(1)}, bf16[256,1024]{1,0:T(8,128)(2,1)}, u32[]{:S(2)}) copy-start(bf16[256,1024]{1,0:T(8,128)(2,1)} %get-tuple-element.19) | copy-start | bytes 1572868

commit v3 on v2

--- a/solution.py
+++ b/solution.py
@@ -48,23 +48,28 @@
         self.zrows = up(self.joined, 8 * depth) // depth
 
     def scratch(self, ring, depth):
-        return [
+        out = [
             pltpu.VMEM((2, self.rows, 128), BF16),
             pltpu.VMEM((self.rows, 128), BF16),
             pltpu.VMEM((self.rows, 128), BF16),
-            pltpu.VMEM((ring - 1, self.first[0], 128), BF16),
-            pltpu.VMEM((ring - 1, self.first[1], 128), BF16),
             pltpu.VMEM((self.first[0], 128), BF16),
             pltpu.VMEM((self.first[1], 128), BF16),
-            pltpu.VMEM((ring - 1, self.second[0], 128), BF16),
-            pltpu.VMEM((ring - 1, self.second[1], 128), BF16),
             pltpu.VMEM((depth * self.zrows, 128), F32),
+            pltpu.VMEM((depth, self.zrows, 128), BF16),
             pltpu.VMEM((depth - 1, self.zrows, 128), BF16),
             pltpu.VMEM((self.zrows, 128), BF16),
             pltpu.VMEM((depth, self.zrows, 128), BF16),
             pltpu.VMEM((2, self.rows, 128), BF16),
-            pltpu.VMEM((depth, self.zrows, 128), BF16),
         ]
+        for sizes in (self.first, self.second):
+            for n in sizes:
+                out += [
+                    pltpu.VMEM((2 * n, 128), BF16),
+                    pltpu.VMEM((n, 128), F32),
+                    pltpu.VMEM((n, 128), BF16),
+                    pltpu.VMEM((n, 128), BF16),
+                ]
+        return out
 
 
 def kernel(ring, depth, terms, dims, *refs):
@@ -78,7 +83,7 @@
      x_v, wr_v, gr, br, wd_v, gd, bd, we_v, ge, be, go_v, label_v,
      pw, perm, back, pre_one, slope_two, gfull, gthree, p_one, p_two, gi_v,
      *rest) = refs
-    n_bufs = 15
+    n_bufs = 27
     bufs = [rest[n_bufs * i : n_bufs * (i + 1)] for i in range(3)]
     load_sem, store_sem, send_sem, recv_sem = rest[3 * n_bufs :]
 
@@ -104,8 +109,8 @@
 
     barrier = pltpu.get_barrier_semaphore()
     greet = [(lat, lon + 1 - 2 * core)]
-    greet += [at_xy((gx + s) % ring, gy) for s in range(1, ring)]
-    greet += [at_xy(gx, (gy + s) % ring) for s in range(1, ring)]
+    greet += [at_xy((gx + s) % ring, gy) for s in (1, ring - 1)]
+    greet += [at_xy(gx, (gy + s) % ring) for s in (1, ring - 1)]
     greet += [((lat + s) % depth, lon) for s in range(1, depth)]
     for dl in (-1, 0, 1):
         for dw in (-1, 1):
@@ -219,116 +224,135 @@
         span = slice(term.start[part], term.start[part] + term.part[part])
         return send(b[0].at[1 - core, span], b[1].at[span], sibling)
 
-    def ring_pos(part, step):
-        return (gx, gy)[part ^ step]
-
-    def ring_dev(part, step, s):
-        if part ^ step == 0:
-            return at_xy((gx + s) % ring, gy)
-        return at_xy(gx, (gy + s) % ring)
-
-    def pair_and_first(t, part, arrived):
+    def halving(axis):
+        at = (gx, gy)[axis]
+        flip, across = at + 1 - 2 * (at % 2), ring - 1 - at
+        high = (1 - core) * (((at + 1) // 2) % 2) + core * (at // 2)
+        low = (1 - core) * (at // 2) + core * (at % 2)
+        near = (1 - core) * flip + core * across
+        far = (1 - core) * across + core * flip
+        devices = [at_xy(p, gy) if axis == 0 else at_xy(gx, p) for p in (near, far)]
+        return high, low, devices
+
+    rings = [halving(0), halving(1)]
+
+    def rows_at(start, n):
+        return pl.ds(pl.multiple_of(start, 16), n)
+
+    def reduction(t, core_copies):
         term, b = terms[t], bufs[t]
-        arrived.wait_recv()
-        lo, n = term.start[part], term.part[part]
-        span = slice(lo, lo + n)
-        b[2][span] = (b[0][core, span].astype(F32) + b[1][span].astype(F32)).astype(BF16)
-        step = term.first[part]
-        out = []
-        for s in range(1, ring):
-            peer = (ring_pos(part, 0) + s) % ring
-            src = b[2].at[pl.ds(pl.multiple_of(lo + peer * step, 16), step)]
-            out.append(send(src, b[3 + part].at[s - 1], ring_dev(part, 0, s)))
-        return out
-
-    def second(t, part, arrived):
-        term, b = terms[t], bufs[t]
+
+        def ring_of(part, step):
+            return rings[part ^ step]
+
+        def quarter(part, step):
+            return (term.first, term.second)[step][part]
+
+        def halves(part, step):
+            at = 11 + 4 * (2 * step + part)
+            return b[at : at + 4]
+
+        def send_half(part, step, src, base):
+            high, _, devices = ring_of(part, step)
+            n = 2 * quarter(part, step)
+            return send(src.at[rows_at(base + (1 - high) * n, n)], halves(part, step)[0], devices[0])
+
+        def send_quarter(part, step, src, base):
+            high, low, devices = ring_of(part, step)
+            n = quarter(part, step)
+            half, kept, sent, got = halves(part, step)
+            mine = base + high * 2 * n
+            for place, to in ((low, kept), (1 - low, sent)):
+                value = src[rows_at(mine + place * n, n)].astype(F32)
+                to[...] = (value + half[rows_at(place * n, n)].astype(F32)).astype(to.dtype)
+            return send(sent, got, devices[1])
+
+        inward = []
+        for part in (0, 1):
+            core_copies[part].wait_recv()
+            span = slice(term.start[part], term.start[part] + term.part[part])
+            b[2][span] = (b[0][core, span].astype(F32) + b[1][span].astype(F32)).astype(BF16)
+            inward.append(send_half(part, 0, b[2], term.start[part]))
+            yield
+        sources = [(b[2], term.start[0]), (b[2], term.start[1])]
+        for step in (0, 1):
+            crossing = []
+            for part in (0, 1):
+                inward[part].wait_recv()
+                crossing.append(send_quarter(part, step, *sources[part]))
+            yield
+            at = 0
+            for part in (0, 1):
+                crossing[part].wait_recv()
+                _, kept, _, got = halves(part, step)
+                total = kept[...] + got[...].astype(F32)
+                if step == 0:
+                    b[3 + part][...] = total.astype(BF16)
+                    sources[part] = (b[3 + part], 0)
+                    inward[part] = send_half(part, 1, *sources[part])
+                else:
+                    n = quarter(part, 1)
+                    b[5][at : at + n] = total
+                    at += n
+            if step == 0:
+                yield
+        if at < depth * term.zrows:
+            b[5][at:] = jnp.zeros((depth * term.zrows - at, 128), F32)
+        b[6][...] = b[5][...].reshape(depth, term.zrows, 128).astype(BF16)
+        arrived = []
+        for s in range(1, depth):
+            peer = (lat + s) % depth
+            arrived.append(send(b[6].at[peer], b[7].at[s - 1], (peer, lon)))
+        yield
         for copy in arrived:
             copy.wait_recv()
-        lo, n = term.start[part], term.first[part]
-        mine = pl.ds(pl.multiple_of(lo + ring_pos(part, 0) * n, 16), n)
-        total = b[2][mine].astype(F32)
-        for s in range(ring - 1):
-            total = total + b[3 + part][s].astype(F32)
-        b[5 + part][...] = total.astype(BF16)
-        step = term.second[part]
-        out = []
-        for s in range(1, ring):
-            peer = (ring_pos(part, 1) + s) % ring
-            src = b[5 + part].at[pl.ds(pl.multiple_of(peer * step, 16), step)]
-            out.append(send(src, b[7 + part].at[s - 1], ring_dev(part, 1, s)))
-        return out
-
-    def third(t, arrived):
-        term, b = terms[t], bufs[t]
-        at = 0
-        for part in (0, 1):
-            for copy in arrived[part]:
-                copy.wait_recv()
-            n = term.second[part]
-            mine = pl.ds(pl.multiple_of(ring_pos(part, 1) * n, 16), n)
-            total = b[5 + part][mine].astype(F32)
-            for s in range(ring - 1):
-                total = total + b[7 + part][s].astype(F32)
-            b[9][at : at + n] = total
-            at += n
-        if at < depth * term.zrows:
-            b[9][at:] = jnp.zeros((depth * term.zrows - at, 128), F32)
-        b[14][...] = b[9][...].reshape(depth, term.zrows, 128).astype(BF16)
-        out = []
-        for s in range(1, depth):
-            peer = (lat + s) % depth
-            out.append(send(b[14].at[peer], b[10].at[s - 1], (peer, lon)))
-        return out
-
-    def fourth(t, arrived):
-        term, b = terms[t], bufs[t]
+        total = b[5][pl.ds(pl.multiple_of(lat * term.zrows, 8), term.zrows)]
+        for s in range(depth - 1):
+            total = total + b[7][s].astype(F32)
+        b[8][...] = total.astype(BF16)
+        b[9][lat] = total.astype(BF16)
+        arrived = [send(b[8], b[9].at[lat], ((lat + s) % depth, lon)) for s in range(1, depth)]
+        yield
         for copy in arrived:
             copy.wait_recv()
-        mine = pl.ds(pl.multiple_of(lat * term.zrows, 8), term.zrows)
-        total = b[9][mine]
-        for s in range(depth - 1):
-            total = total + b[10][s].astype(F32)
-        b[11][...] = total.astype(BF16)
-        b[12][lat] = total.astype(BF16)
-        return [
-            send(b[11], b[12].at[lat], ((lat + s) % depth, lon)) for s in range(1, depth)
-        ]
-
-    def fifth(t, arrived):
-        term, b = terms[t], bufs[t]
-        for copy in arrived:
+        at = 0
+        whole = b[9][...].astype(F32).reshape(depth * term.zrows, 128)
+        final = b[10].at[core]
+        base, crossing = [], []
+        for part in (0, 1):
+            high, low, _ = ring_of(part, 0)
+            base.append(term.start[part] + (2 * high + low) * quarter(part, 0))
+            high, low, devices = ring_of(part, 1)
+            n = quarter(part, 1)
+            here = rows_at(base[part] + (2 * high + low) * n, n)
+            b[10][core, here] = whole[at : at + n].astype(BF16)
+            at += n
+            crossing.append(send(final.at[here], final.at[here], devices[1]))
+        yield
+        for step in (1, 0):
+            outward = []
+            for part in (0, 1):
+                crossing[part].wait_recv()
+                high, _, devices = ring_of(part, step)
+                n = 2 * quarter(part, step)
+                start = base[part] if step == 1 else term.start[part]
+                here = rows_at(start + high * n, n)
+                outward.append(send(final.at[here], final.at[here], devices[0]))
+            yield
+            crossing = []
+            for part in (0, 1):
+                outward[part].wait_recv()
+                if step == 1:
+                    here = rows_at(base[part], quarter(part, 0))
+                    device = ring_of(part, 0)[2][1]
+                else:
+                    here = slice(term.start[part], term.start[part] + term.part[part])
+                    device = sibling
+                crossing.append(send(final.at[here], final.at[here], device))
+            yield
+        for copy in crossing:
             copy.wait_recv()
-        at, outs = 0, []
-        whole = b[12][...].astype(F32).reshape(depth * term.zrows, 128)
-        for part in (0, 1):
-            n = term.second[part]
-            place = term.start[part] + ring_pos(part, 0) * term.first[part] + ring_pos(part, 1) * n
-            here = pl.ds(pl.multiple_of(place, 16), n)
-            b[13][core, here] = whole[at : at + n].astype(BF16)
-            at += n
-            block = b[13].at[core, here]
-            outs.append([send(block, block, ring_dev(part, 1, s)) for s in range(1, ring)])
-        return outs
-
-    def sixth(t, arrived):
-        term, b = terms[t], bufs[t]
-        outs = []
-        for part in (0, 1):
-            for copy in arrived[part]:
-                copy.wait_recv()
-            n = term.first[part]
-            place = term.start[part] + ring_pos(part, 0) * n
-            block = b[13].at[core, pl.ds(pl.multiple_of(place, 16), n)]
-            outs.append([send(block, block, ring_dev(part, 0, s)) for s in range(1, ring)])
-        return outs
-
-    def seventh(t, arrived):
-        b = bufs[t]
-        for part in (0, 1):
-            for copy in arrived[part]:
-                copy.wait_recv()
-        return send(b[13].at[core], b[13].at[core], sibling)
+        yield
 
     stores = []
 
@@ -388,64 +412,63 @@
     for j in range(blocks):
         put_term(0, j * 256, dot_lt(mid_two, gthree[:, j * 256 : (j + 1) * 256]))
     e_core = [core_send(0, 0), core_send(0, 1)]
+    d_core, r_core = [], []
+    e_sum, d_sum, r_sum = reduction(0, e_core), reduction(1, d_core), reduction(2, r_core)
+
+    def advance(*sums):
+        for gen in sums:
+            next(gen)
+
     center = tap(p_two, 1, 1)
     taps_a = terms[1].ra // chan_mid
-    d_core = []
     for i in range(9):
         put_term(1, i * chan_mid, dot_lt(tap(p_one, i // 3, i % 3), center))
         if i == taps_a - 1:
             d_core.append(core_send(1, 0))
-            e_first = [pair_and_first(0, part, e_core[part]) for part in (0, 1)]
+            advance(e_sum, e_sum)
     d_core.append(core_send(1, 1))
+    advance(d_sum)
 
     total = dot_rt(center, wd_v[4])
     wait_two()
     for i in (0, 1, 2, 3, 5, 6, 7, 8):
         total = total + dot_rt(tap(p_two, 2 - i // 3, 2 - i % 3), wd_v[i])
+        if i == 3:
+            advance(d_sum, e_sum)
     grad_one = (to_natural(total) * slope(pre_one[...]) * gr[...]).astype(BF16)
-    r_core = []
     for j in range(2):
         half = chan_in // 2
         put_term(2, j * half, dot_lt(x_v[:, j * half : (j + 1) * half], grad_one))
         r_core.append(core_send(2, j))
-    d_first = [pair_and_first(1, part, d_core[part]) for part in (0, 1)]
-    e_second = [second(0, part, e_first[part]) for part in (0, 1)]
+        if j == 0:
+            advance(e_sum, d_sum)
     for j in range(blocks):
         cols = slice(j * 256, (j + 1) * 256)
         gi_v[:, cols] = (dot_rt(grad_one, wr_v[cols, :]) + gfull[:, cols]).astype(BF16)
+        if j == 1:
+            advance(r_sum, r_sum, e_sum, d_sum)
     store(gi_v, gi_hbm)
-    r_first = [pair_and_first(2, part, r_core[part]) for part in (0, 1)]
-    e_third = third(0, e_second)
-    d_second = [second(1, part, d_first[part]) for part in (0, 1)]
-    r_second = [second(2, part, r_first[part]) for part in (0, 1)]
-    d_third = third(1, d_second)
-    e_fourth = fourth(0, e_third)
-    r_third = third(2, r_second)
-    d_fourth = fourth(1, d_third)
-    e_fifth = fifth(0, e_fourth)
-    r_fourth = fourth(2, r_third)
-    d_fifth = fifth(1, d_fourth)
-    e_sixth = sixth(0, e_fifth)
-    r_fifth = fifth(2, r_fourth)
-    d_sixth = sixth(1, d_fifth)
-    e_last = seventh(0, e_sixth)
-    r_sixth = sixth(2, r_fifth)
-    d_last = seventh(1, d_sixth)
-    r_last = seventh(2, r_sixth)
-
-    e_last.wait_recv()
-    for side in (0, 1):
-        for j in range(blocks):
-            first = j * 256 + side * 128
-            store(
-                bufs[0][13].at[side, j * 256 : (j + 1) * 256], gexp_hbm.at[:, first : first + 128]
-            )
-    d_last.wait_recv()
-    for side in (0, 1):
-        store(bufs[1][13].at[side], gdil_hbm.at[:, side * 128 : (side + 1) * 128])
-    r_last.wait_recv()
-    for side in (0, 1):
-        store(bufs[2][13].at[side], gred_hbm.at[:, side * 128 : (side + 1) * 128])
+    done = {id(e_sum): 5, id(d_sum): 4, id(r_sum): 2}
+    n_stages = 13
+    order = [e_sum, d_sum, r_sum]
+    while any(done[id(gen)] < n_stages for gen in order):
+        for gen in order:
+            if done[id(gen)] < n_stages:
+                advance(gen)
+                done[id(gen)] += 1
+                if done[id(gen)] == n_stages:
+                    if gen is e_sum:
+                        for side in (0, 1):
+                            for j in range(blocks):
+                                first = j * 256 + side * 128
+                                store(
+                                    bufs[0][10].at[side, j * 256 : (j + 1) * 256],
+                                    gexp_hbm.at[:, first : first + 128],
+                                )
+                    else:
+                        t, out = (1, gdil_hbm) if gen is d_sum else (2, gred_hbm)
+                        for side in (0, 1):
+                            store(bufs[t][10].at[side], out.at[:, side * 128 : (side + 1) * 128])
     halo_copies = {id(copy) for _, copy, _ in guarded}
     for dl, copy, on in guarded:
         on(dl, False, copy.wait_send)

time: 68.9 us -> 82.3 us (1.19)
  Pallas kernels: 62.7 us -> 76.1 us
    pallas_call x1, Pallas kernels: 62.7 us -> 76.1 us  [per_device(): pl.pallas_call(functools.partial(kernel, ring, depth, terms, (batch, heig...]
where the time goes in v3:
time: 82.3 us; the launch traced here: 82.1 us
  Pallas kernels  76.1 us (92%)
  local copies, waits for them, and re-layouts  5.38 us (7%)
    pallas_call x1, Pallas kernels, per_device(): pl.pallas_call(functools.partial(kernel, ring, depth, terms, (batch, heig...  76.1 us
    unnamed x10, local copies, waits for them, and re-layouts  5.38 us

profile of v3, /device:TPU:1, one launch (start us, length us, event | category | flops | bytes accessed | tf_op | source)
XLA Modules:
  0.0 82.1 jit_solution(6858941851855688519)
XLA Ops:
  0.6 76.1 %shard_map.156 = (bf16[512,1024]{1,0:T(8,128)(2,1)}, bf16[1024,256]{1,0:T(8,128)(2,1)}, bf16[2304,256]{1,0:T(8,128)(2,1)}, bf16[256,1024]{1,0:T(8,128)(2,1)}) custom-call(bf16[512,1024]{1,0:T(8,128)(2,1)} %bitcast.18, bf16[1024,256]{1,0:T(8,128)(2,1)} %refs_1_.1, f32[1,256]{1,0:T(1,128)} %bitcast.23, f32[1,256]{1,0:T(1,128)} %bitcast.24, ...), custom_call_target="tpu_custom_call" | custom-call | tf_op jit(solution)/shard_map/pallas_call | solution.py:543
  76.7 0.0 copy-start.2
  76.7 0.0 copy-start
  76.7 2.4 %copy.21 = bf16[4,16,8,1024]{3,2,1,0:T(8,128)(2,1)} copy(bf16[4,16,8,1024]{3,2,1,0:T(8,128)(2,1)} %bitcast.17) | data formatting | bytes 2097152
  79.1 0.0 copy-done.2
  79.1 0.8 copy.22
  79.9 0.0 copy-done
  79.9 0.0 copy-start.1
  79.9 1.0 %copy.23 = bf16[3,3,256,256]{3,2,1,0:T(8,128)(2,1)} copy(bf16[3,3,256,256]{3,2,1,0:T(8,128)(2,1)S(1)} %bitcast.15) | data formatting | bytes 2359296
  80.9 0.4 copy-done.1
  81.3 0.8 copy.24
Async XLA Ops:
  76.7 2.4 %copy-start.2 = (bf16[1024,256]{1,0:T(8,128)(2,1)S(1)}, bf16[1024,256]{1,0:T(8,128)(2,1)}, u32[]{:S(2)}) copy-start(bf16[1024,256]{1,0:T(8,128)(2,1)} %get-tuple-element.17) | copy-start | bytes 1572868
  76.7 3.2 %copy-start = (bf16[2304,256]{1,0:T(8,128)(2,1)S(1)}, bf16[2304,256]{1,0:T(8,128)(2,1)}, u32[]{:S(2)}) copy-start(bf16[2304,256]{1,0:T(8,128)(2,1)} %get-tuple-element.10) | copy-start | bytes 3538948
  79.9 1.4 %copy-start.1 = (bf16[256,1024]{1,0:T(8,128)(2,1)S(1)}, bf16[256,1024]{1,0:T(8,128)(2,1)}, u32[]{:S(2)}) copy-start(bf16[256,1024]{1,0:T(8,128)(2,1)} %get-tuple-element.19) | copy-start | bytes 1572868

commit v4 on v2

--- a/solution.py
+++ b/solution.py
@@ -313,7 +313,7 @@
 
     def sixth(t, arrived):
         term, b = terms[t], bufs[t]
-        outs = []
+        outs, across = [], []
         for part in (0, 1):
             for copy in arrived[part]:
                 copy.wait_recv()
@@ -321,14 +321,32 @@
             place = term.start[part] + ring_pos(part, 0) * n
             block = b[13].at[core, pl.ds(pl.multiple_of(place, 16), n)]
             outs.append([send(block, block, ring_dev(part, 0, s)) for s in range(1, ring)])
-        return outs
-
-    def seventh(t, arrived):
-        b = bufs[t]
-        for part in (0, 1):
-            for copy in arrived[part]:
-                copy.wait_recv()
-        return send(b[13].at[core], b[13].at[core], sibling)
+            across.append(send(block, block, sibling))
+        return outs, across
+
+    def seventh(t, arrived, out, blocks):
+        term, b = terms[t], bufs[t]
+        outs, across = arrived
+        for s in range(1, ring):
+            for part in (0, 1):
+                outs[part][s - 1].wait_recv()
+                n = term.first[part]
+                place = term.start[part] + ((ring_pos(part, 0) + ring - s) % ring) * n
+                block = b[13].at[core, pl.ds(pl.multiple_of(place, 16), n)]
+                across.append(send(block, block, sibling))
+        store_side(t, core, out, blocks)
+        return across
+
+    def last(t, across, out, blocks):
+        for copy in across:
+            copy.wait_recv()
+        store_side(t, 1 - core, out, blocks)
+
+    def store_side(t, side, out, blocks):
+        rows = terms[t].rows // blocks
+        for j in range(blocks):
+            cols = pl.ds(pl.multiple_of(j * 256 + side * 128, 128), 128)
+            store(bufs[t][13].at[side, j * rows : (j + 1) * rows], out.at[:, cols])
 
     stores = []
 
@@ -410,13 +428,19 @@
         r_core.append(core_send(2, j))
     d_first = [pair_and_first(1, part, d_core[part]) for part in (0, 1)]
     e_second = [second(0, part, e_first[part]) for part in (0, 1)]
-    for j in range(blocks):
+
+    def input_grad(j):
         cols = slice(j * 256, (j + 1) * 256)
         gi_v[:, cols] = (dot_rt(grad_one, wr_v[cols, :]) + gfull[:, cols]).astype(BF16)
-    store(gi_v, gi_hbm)
+
+    input_grad(0)
     r_first = [pair_and_first(2, part, r_core[part]) for part in (0, 1)]
     e_third = third(0, e_second)
+    input_grad(1)
     d_second = [second(1, part, d_first[part]) for part in (0, 1)]
+    for j in range(2, blocks):
+        input_grad(j)
+    store(gi_v, gi_hbm)
     r_second = [second(2, part, r_first[part]) for part in (0, 1)]
     d_third = third(1, d_second)
     e_fourth = fourth(0, e_third)
@@ -428,24 +452,13 @@
     e_sixth = sixth(0, e_fifth)
     r_fifth = fifth(2, r_fourth)
     d_sixth = sixth(1, d_fifth)
-    e_last = seventh(0, e_sixth)
+    e_last = seventh(0, e_sixth, gexp_hbm, blocks)
     r_sixth = sixth(2, r_fifth)
-    d_last = seventh(1, d_sixth)
-    r_last = seventh(2, r_sixth)
-
-    e_last.wait_recv()
-    for side in (0, 1):
-        for j in range(blocks):
-            first = j * 256 + side * 128
-            store(
-                bufs[0][13].at[side, j * 256 : (j + 1) * 256], gexp_hbm.at[:, first : first + 128]
-            )
-    d_last.wait_recv()
-    for side in (0, 1):
-        store(bufs[1][13].at[side], gdil_hbm.at[:, side * 128 : (side + 1) * 128])
-    r_last.wait_recv()
-    for side in (0, 1):
-        store(bufs[2][13].at[side], gred_hbm.at[:, side * 128 : (side + 1) * 128])
+    d_last = seventh(1, d_sixth, gdil_hbm, 1)
+    last(0, e_last, gexp_hbm, blocks)
+    r_last = seventh(2, r_sixth, gred_hbm, 1)
+    last(1, d_last, gdil_hbm, 1)
+    last(2, r_last, gred_hbm, 1)
     halo_copies = {id(copy) for _, copy, _ in guarded}
     for dl, copy, on in guarded:
         on(dl, False, copy.wait_send)
@@ -508,7 +521,7 @@
     ]
     for term in terms:
         scratch += term.scratch(ring, depth)
-    n_remote = 16 + 3 * (2 + 8 * (ring - 1) + 2 * (depth - 1) + 1)
+    n_remote = 16 + 3 * (2 + 8 * (ring - 1) + 2 * (depth - 1) + 2 * ring)
     scratch += [
         pltpu.SemaphoreType.DMA((12,)),
         pltpu.SemaphoreType.DMA((2 * (chan_in // 256) + 5,)),

time: 68.9 us -> 69.1 us (level)
  no operation moved by 1% of the time
where the time goes in v4:
time: 69.1 us; the launch traced here: 68.9 us
  Pallas kernels  62.8 us (91%)
  local copies, waits for them, and re-layouts  5.38 us (8%)
    pallas_call x1, Pallas kernels, per_device(): pl.pallas_call(functools.partial(kernel, ring, depth, terms, (batch, heig...  62.8 us
    unnamed x10, local copies, waits for them, and re-layouts  5.38 us

profile of v4, /device:TPU:1, one launch (start us, length us, event | category | flops | bytes accessed | tf_op | source)
XLA Modules:
  0.0 68.9 jit_solution(14377279245404124575)
XLA Ops:
  0.6 62.8 %shard_map.156 = (bf16[512,1024]{1,0:T(8,128)(2,1)}, bf16[1024,256]{1,0:T(8,128)(2,1)}, bf16[2304,256]{1,0:T(8,128)(2,1)}, bf16[256,1024]{1,0:T(8,128)(2,1)}) custom-call(bf16[512,1024]{1,0:T(8,128)(2,1)} %bitcast.18, bf16[1024,256]{1,0:T(8,128)(2,1)} %refs_1_.1, f32[1,256]{1,0:T(1,128)} %bitcast.23, f32[1,256]{1,0:T(1,128)} %bitcast.24, ...), custom_call_target="tpu_custom_call" | custom-call | tf_op jit(solution)/shard_map/pallas_call | solution.py:533
  63.5 0.0 copy-start.2
  63.5 0.0 copy-start
  63.5 2.4 %copy.21 = bf16[4,16,8,1024]{3,2,1,0:T(8,128)(2,1)} copy(bf16[4,16,8,1024]{3,2,1,0:T(8,128)(2,1)} %bitcast.17) | data formatting | bytes 2097152
  65.9 0.0 copy-done.2
  65.9 0.8 %copy.22 = bf16[1024,256]{1,0:T(8,128)(2,1)} copy(bf16[1024,256]{1,0:T(8,128)(2,1)S(1)} %copy-done.2) | data formatting | bytes 1048576
  66.7 0.0 copy-done
  66.7 0.0 copy-start.1
  66.7 1.0 %copy.23 = bf16[3,3,256,256]{3,2,1,0:T(8,128)(2,1)} copy(bf16[3,3,256,256]{3,2,1,0:T(8,128)(2,1)S(1)} %bitcast.15) | data formatting | bytes 2359296
  67.7 0.4 copy-done.1
  68.1 0.8 %copy.24 = bf16[256,1024]{1,0:T(8,128)(2,1)} copy(bf16[256,1024]{1,0:T(8,128)(2,1)S(1)} %copy-done.1) | data formatting | bytes 1048576
Async XLA Ops:
  63.5 2.4 %copy-start.2 = (bf16[1024,256]{1,0:T(8,128)(2,1)S(1)}, bf16[1024,256]{1,0:T(8,128)(2,1)}, u32[]{:S(2)}) copy-start(bf16[1024,256]{1,0:T(8,128)(2,1)} %get-tuple-element.17) | copy-start | bytes 1572868
  63.5 3.2 %copy-start = (bf16[2304,256]{1,0:T(8,128)(2,1)S(1)}, bf16[2304,256]{1,0:T(8,128)(2,1)}, u32[]{:S(2)}) copy-start(bf16[2304,256]{1,0:T(8,128)(2,1)} %get-tuple-element.10) | copy-start | bytes 3538948
  66.7 1.4 %copy-start.1 = (bf16[256,1024]{1,0:T(8,128)(2,1)S(1)}, bf16[256,1024]{1,0:T(8,128)(2,1)}, u32[]{:S(2)}) copy-start(bf16[256,1024]{1,0:T(8,128)(2,1)} %get-tuple-element.19) | copy-start | bytes 1572868

commit v5 on v2

--- a/solution.py
+++ b/solution.py
@@ -399,16 +399,18 @@
     d_core.append(core_send(1, 1))
 
     total = dot_rt(center, wd_v[4])
+    d_first = [pair_and_first(1, 0, d_core[0])]
     wait_two()
     for i in (0, 1, 2, 3, 5, 6, 7, 8):
         total = total + dot_rt(tap(p_two, 2 - i // 3, 2 - i % 3), wd_v[i])
+        if i == 3:
+            d_first.append(pair_and_first(1, 1, d_core[1]))
     grad_one = (to_natural(total) * slope(pre_one[...]) * gr[...]).astype(BF16)
     r_core = []
     for j in range(2):
         half = chan_in // 2
         put_term(2, j * half, dot_lt(x_v[:, j * half : (j + 1) * half], grad_one))
         r_core.append(core_send(2, j))
-    d_first = [pair_and_first(1, part, d_core[part]) for part in (0, 1)]
     e_second = [second(0, part, e_first[part]) for part in (0, 1)]
     for j in range(blocks):
         cols = slice(j * 256, (j + 1) * 256)

time: 68.9 us -> 66.2 us (0.961)
  Pallas kernels: 62.7 us -> 59.9 us
    pallas_call x1, Pallas kernels: 62.7 us -> 59.9 us  [per_device(): pl.pallas_call(functools.partial(kernel, ring, depth, terms, (batch, heig...]
where the time goes in v5:
time: 66.2 us; the launch traced here: 66 us
  Pallas kernels  59.9 us (90%)
  local copies, waits for them, and re-layouts  5.38 us (8%)
    pallas_call x1, Pallas kernels, per_device(): pl.pallas_call(functools.partial(kernel, ring, depth, terms, (batch, heig...  59.9 us
    unnamed x10, local copies, waits for them, and re-layouts  5.38 us

profile of v5, /device:TPU:1, one launch (start us, length us, event | category | flops | bytes accessed | tf_op | source)
XLA Modules:
  0.0 66.0 jit_solution(12251806126045421625)
XLA Ops:
  0.6 59.9 %shard_map.156 = (bf16[512,1024]{1,0:T(8,128)(2,1)}, bf16[1024,256]{1,0:T(8,128)(2,1)}, bf16[2304,256]{1,0:T(8,128)(2,1)}, bf16[256,1024]{1,0:T(8,128)(2,1)}) custom-call(bf16[512,1024]{1,0:T(8,128)(2,1)} %bitcast.18, bf16[1024,256]{1,0:T(8,128)(2,1)} %refs_1_.1, f32[1,256]{1,0:T(1,128)} %bitcast.23, f32[1,256]{1,0:T(1,128)} %bitcast.24, ...), custom_call_target="tpu_custom_call" | custom-call | tf_op jit(solution)/shard_map/pallas_call | solution.py:522
  60.6 0.0 copy-start.2
  60.6 0.0 copy-start
  60.6 2.4 %copy.21 = bf16[4,16,8,1024]{3,2,1,0:T(8,128)(2,1)} copy(bf16[4,16,8,1024]{3,2,1,0:T(8,128)(2,1)} %bitcast.17) | data formatting | bytes 2097152
  63.0 0.0 copy-done.2
  63.0 0.8 %copy.22 = bf16[1024,256]{1,0:T(8,128)(2,1)} copy(bf16[1024,256]{1,0:T(8,128)(2,1)S(1)} %copy-done.2) | data formatting | bytes 1048576
  63.8 0.0 copy-done
  63.8 0.0 copy-start.1
  63.8 1.0 %copy.23 = bf16[3,3,256,256]{3,2,1,0:T(8,128)(2,1)} copy(bf16[3,3,256,256]{3,2,1,0:T(8,128)(2,1)S(1)} %bitcast.15) | data formatting | bytes 2359296
  64.8 0.4 copy-done.1
  65.2 0.8 %copy.24 = bf16[256,1024]{1,0:T(8,128)(2,1)} copy(bf16[256,1024]{1,0:T(8,128)(2,1)S(1)} %copy-done.1) | data formatting | bytes 1048576
Async XLA Ops:
  60.6 2.4 %copy-start.2 = (bf16[1024,256]{1,0:T(8,128)(2,1)S(1)}, bf16[1024,256]{1,0:T(8,128)(2,1)}, u32[]{:S(2)}) copy-start(bf16[1024,256]{1,0:T(8,128)(2,1)} %get-tuple-element.17) | copy-start | bytes 1572868
  60.6 3.2 %copy-start = (bf16[2304,256]{1,0:T(8,128)(2,1)S(1)}, bf16[2304,256]{1,0:T(8,128)(2,1)}, u32[]{:S(2)}) copy-start(bf16[2304,256]{1,0:T(8,128)(2,1)} %get-tuple-element.10) | copy-start | bytes 3538948
  63.8 1.4 %copy-start.1 = (bf16[256,1024]{1,0:T(8,128)(2,1)S(1)}, bf16[256,1024]{1,0:T(8,128)(2,1)}, u32[]{:S(2)}) copy-start(bf16[256,1024]{1,0:T(8,128)(2,1)} %get-tuple-element.19) | copy-start | bytes 1572868
